TPU v7x, 32 devices: a whole 2x2x4 slice. The times are simulated.
32 devices in a mesh: groups: 2 (over x), wide: 8 (over z, y), narrow: 2 (over core).
Axes of the slice: x: 2, y: 2, z: 4, core: 2. Of those that a mesh axis runs over, the one named last changes fastest.
Arguments:
- features: bfloat16 [64, 16, 128, 256], P(('groups', 'wide'), 'narrow'), parts along dimension 0, may hold values from -6 to 6
- tile_ids: int32 [64, 16, 3], P(('groups', 'wide'), 'narrow'), parts along dimension 0, may hold values from 0 to 15
- tiles: bfloat16 [16, 128, 128], replicated, may hold values from -0.25 to 0.25
- w_first: bfloat16 [256, 256], replicated, may hold values from -0.375 to 0.375
- w_second: bfloat16 [256, 256], replicated, may hold values from -0.375 to 0.375
- readout: bfloat16 [256], replicated, may hold values from -0.375 to 0.375
- target: float32 [64, 16, 128], P(('groups', 'wide'), 'narrow'), parts along dimension 0, may hold values from -6 to 6
Outputs:
- pred: float32 [64, 16, 128], P(('groups', 'wide'), 'narrow'), parts along dimension 0
- grad_first: float32 [512, 256], P(('groups', 'wide', 'narrow')), parts along dimension 0
- grad_second: float32 [512, 256], P(('groups', 'wide', 'narrow')), parts along dimension 0
- grad_readout: float32 [512], P('groups'), parts along dimension 0
There are 2 independent parts, one for each index of `groups`. A program takes and returns all parts, laid end to end along the dimension named above; an argument that names none is the same for every part. Nothing has to cross between parts.
All inputs are finite; a program needn't handle non-finite values.
Results may differ from a plain program's by a relative error of at most 0.0049.
Values may be sent and summed in bfloat16 or wider, within the bound.
No kernel may reach another device: no remote copies, remote signals or barrier semaphores. Data moves between devices by JAX's collectives and lax.ppermute only.
A program may use at most 128 MiB of HBM per device.

v0:
```python
import jax
import jax.numpy as jnp
from jax import lax
from jax.sharding import PartitionSpec as P


def extended(cells, sides, width):
    for axis, dim in sides:
        count = lax.axis_size(axis)
        ends = count - 1
        head = lax.slice_in_dim(cells, 0, width, axis=dim)
        tail = lax.slice_in_dim(cells, cells.shape[dim] - width, cells.shape[dim], axis=dim)
        cells = jnp.concatenate(
            [
                lax.ppermute(tail, axis, [(i, (i + 1) % count) for i in range(ends)]),
                cells,
                lax.ppermute(head, axis, [((i + 1) % count, i) for i in range(ends)]),
            ],
            axis=dim,
        )
    return cells


def shifted(block, axis, distance):
    devices = range(lax.axis_size(axis))
    route = [(i - distance, i) for i in devices if i - distance in devices]
    return lax.ppermute(block, axis, route)


def apply_operator(padded, ids_pad, tiles, offset):
    nx = padded.shape[0] - 2
    ny = padded.shape[1] - 2
    centre_ids = ids_pad[offset + 1 : offset + 1 + nx, offset + 1 : offset + 1 + ny]
    west_ids = ids_pad[offset : offset + nx, offset + 1 : offset + 1 + ny, 1]
    south_ids = ids_pad[offset + 1 : offset + 1 + nx, offset : offset + ny, 2]
    centre = padded[1:-1, 1:-1]
    selfs = jnp.take(tiles, centre_ids[..., 0], axis=0)
    total = jnp.einsum("xynm,xymh->xynh", selfs, centre, preferred_element_type=jnp.float32)
    total = total + jnp.einsum("xymn,xymh->xynh", selfs, centre, preferred_element_type=jnp.float32)
    east = jnp.take(tiles, centre_ids[..., 1], axis=0)
    total = total + jnp.einsum(
        "xynm,xymh->xynh", east, padded[2:, 1:-1], preferred_element_type=jnp.float32
    )
    west = jnp.take(tiles, west_ids, axis=0)
    total = total + jnp.einsum(
        "xymn,xymh->xynh", west, padded[:-2, 1:-1], preferred_element_type=jnp.float32
    )
    north = jnp.take(tiles, centre_ids[..., 2], axis=0)
    total = total + jnp.einsum(
        "xynm,xymh->xynh", north, padded[1:-1, 2:], preferred_element_type=jnp.float32
    )
    south = jnp.take(tiles, south_ids, axis=0)
    total = total + jnp.einsum(
        "xymn,xymh->xynh", south, padded[1:-1, :-2], preferred_element_type=jnp.float32
    )
    return total


def edge_rim(field):
    return extended(field, (("wide", 0), ("narrow", 1)), 1)


def column_term(matrix, grads):
    return lax.dot_general(
        matrix, grads, (((0,), (0,)), ((), ())), preferred_element_type=jnp.float32
    )


def per_device(features, tile_ids, tiles, w_first, w_second, readout, target):
    bx = features.shape[0]
    by = features.shape[1]
    width = features.shape[3]
    west_rim = shifted(tile_ids[bx - 1, :, 1], "wide", 1)
    south_rim = shifted(tile_ids[:, by - 1, 2], "narrow", 1)
    ids_pad = jnp.zeros((bx + 2, by + 2, 3), jnp.int32)
    ids_pad = ids_pad.at[1 : 1 + bx, 1 : 1 + by].set(tile_ids)
    ids_pad = ids_pad.at[0, 1 : 1 + by, 1].set(west_rim)
    ids_pad = ids_pad.at[1 : 1 + bx, 0, 2].set(south_rim)
    id_off = 0
    m_one = apply_operator(edge_rim(features), ids_pad, tiles, id_off).astype(jnp.bfloat16)
    z_one = jnp.einsum("xynh,hk->xynk", m_one, w_first, preferred_element_type=jnp.float32)
    x_one = (features.astype(jnp.float32) + jnp.tanh(z_one)).astype(jnp.bfloat16)
    m_two = apply_operator(edge_rim(x_one), ids_pad, tiles, id_off).astype(jnp.bfloat16)
    z_two = jnp.einsum("xynh,hk->xynk", m_two, w_second, preferred_element_type=jnp.float32)
    x_two = (x_one.astype(jnp.float32) + jnp.tanh(z_two)).astype(jnp.bfloat16)
    readf = readout.astype(jnp.float32)
    pred = jnp.einsum("xynh,h->xyn", x_two, readout, preferred_element_type=jnp.float32)
    nodes = bx * by * features.shape[2] * lax.axis_size("wide") * lax.axis_size("narrow")
    scale = jnp.sqrt(jnp.float32(width) / jnp.float32(nodes))
    grad_pred = (pred - target) * scale
    local_readout = jnp.einsum("xynh,xyn->h", x_two.astype(jnp.float32), grad_pred)
    grad_readout = lax.psum(local_readout, ("wide", "narrow"))
    grad_x_two = grad_pred[..., None] * readf
    tanh_two = jnp.tanh(z_two)
    grad_z_two = (grad_x_two * (1.0 - tanh_two * tanh_two)).astype(jnp.bfloat16)
    m_two_flat = m_two.reshape(-1, width)
    m_one_flat = m_one.reshape(-1, width)
    gz_two_flat = grad_z_two.reshape(-1, width)
    grad_second = lax.psum_scatter(
        column_term(m_two_flat, gz_two_flat), ("wide", "narrow"), scatter_dimension=0, tiled=True
    )
    grad_m_two = jnp.einsum(
        "xynk,hk->xynh", grad_z_two, w_second, preferred_element_type=jnp.float32
    ).astype(jnp.bfloat16)
    grad_pad = extended(grad_m_two, (("wide", 0), ("narrow", 1)), 1)
    grad_x_one = grad_x_two + apply_operator(grad_pad, ids_pad, tiles, id_off)
    tanh_one = jnp.tanh(z_one)
    grad_z_one = (grad_x_one * (1.0 - tanh_one * tanh_one)).astype(jnp.bfloat16)
    gz_one_flat = grad_z_one.reshape(-1, width)
    grad_first = lax.psum_scatter(
        column_term(m_one_flat, gz_one_flat), ("wide", "narrow"), scatter_dimension=0, tiled=True
    )
    return (pred, grad_first, grad_second, grad_readout)


def solution(mesh):
    in_specs = (
        P(("groups", "wide"), "narrow", None, None),
        P(("groups", "wide"), "narrow", None),
        P(),
        P(),
        P(),
        P(),
        P(("groups", "wide"), "narrow", None),
    )
    out_specs = (
        P(("groups", "wide"), "narrow", None),
        P(("groups", "wide", "narrow"), None),
        P(("groups", "wide", "narrow"), None),
        P("groups"),
    )
    return jax.shard_map(
        per_device, mesh=mesh, in_specs=in_specs, out_specs=out_specs, check_vma=False
    )
```

profile of v0, /device:TPU:0, one launch (start us, length us, event | category | flops | bytes accessed | tf_op | source)
XLA Modules:
  0.0 255.8 jit_solution(11594053089742596315)
XLA Ops:
  8.0 4.9 %collective-permute-start = (s32[8]{0:T(128)S(1)}, s32[8]{0:T(128)S(1)}, u32[]{:S(2)}, u32[]{:S(2)}) collective-permute-start(s32[8]{0:T(128)S(1)} %slice_bitcast_fusion.5), channel_id=1, source_target_pairs={{0,2},{2,4},{4,6},{6,8},{8,10},{10,12},{12,14},{1,3},{3,5},{5,7},{... | collective-permute-start | bytes 104 | tf_op jit(solution)/shard_map/ppermute | solution.py:27
  13.7 1.5 collective-permute-start.1
  15.2 2.3 fusion.94
  17.5 3.4 %collective-permute-start.3 = (bf16[1,8,128,256]{3,2,1,0:T(8,128)(2,1)}, bf16[1,8,128,256]{3,2,1,0:T(8,128)(2,1)S(1)}, u32[]{:S(2)}, u32[]{:S(2)}) collective-permute-start(bf16[1,8,128,256]{3,2,1,0:T(8,128)(2,1)} %get-tuple-element.52), channel_id=1, source_target_pairs={{0,2},{2,4},{4,6},{6,8},{8,10},{10,12},{12,14},{1,3},{3,5},{5,7},{... | collective-permute-start | bytes 1572872 | tf_op jit(solution)/shard_map/ppermute | solution.py:15
  20.9 1.3 collective-permute-start.2
  24.8 1.7 gather_fusion
  26.5 2.2 copy.13
  28.8 4.0 %fusion.46 = f32[4,8,128,256]{3,2,1,0:T(8,128)} fusion(bf16[4,8,128,256]{3,2,1,0:T(8,128)(2,1)S(1)} %copy-done.2, bf16[4,8,128,128]{2,3,1,0:T(8,128)(2,1)} %copy.13, pred[4,8]{1,0:T(4,128)(4,1)S(1)} %get-tuple-element.57), kind=kOutput, calls=%fused_computation.83 | convolution fusion | flops 268959744 | bytes 7340064 | tf_op jit(solution)/shard_map/xymn,xymh->xynh/dot_general | solution.py:39
  32.7 1.6 gather_fusion.3
  34.5 1.7 gather_fusion.2
  36.2 2.3 copy.15
  38.5 1.7 gather_fusion.1
  40.2 1.7 gather_fusion.4
  41.8 2.3 copy.16
  44.1 4.4 %fusion.47 = f32[4,8,128,256]{3,2,1,0:T(8,128)} fusion(bf16[4,8,128,256]{3,2,1,0:T(8,128)(2,1)S(1)} %copy-done.2, bf16[4,8,128,128]{2,3,1,0:T(8,128)(2,1)} %copy.13, pred[4,8]{1,0:T(4,128)(4,1)S(1)} %get-tuple-element.57), kind=kOutput, calls=%fused_computation.84 | convolution fusion | flops 268959744 | bytes 7340064 | tf_op jit(solution)/shard_map/xynm,xymh->xynh/dot_general | solution.py:38
  49.9 1.3 collective-permute-start.4
  51.2 3.1 %collective-permute-start.5 = (bf16[6,1,128,256]{3,2,1,0:T(8,128)(2,1)S(1)}, bf16[6,1,128,256]{3,2,1,0:T(8,128)(2,1)S(1)}, u32[]{:S(2)}, u32[]{:S(2)}) collective-permute-start(bf16[6,1,128,256]{3,2,1,0:T(8,128)(2,1)S(1)} %get-tuple-element.45), channel_id=1, source_target_pairs={{0,1},{2,3},{4,5},{6,7},{8,9},{10,11},{12,13},{14,15},{16,17},{18,... | collective-permute-start | bytes 1179656 | tf_op jit(solution)/shard_map/ppermute | solution.py:15
  55.6 1.9 fusion.25
  57.5 2.9 %fusion.21 = f32[4,8,128,256]{3,2,1,0:T(8,128)} fusion(bf16[6,1,128,256]{3,2,1,0:T(8,128)(2,1)S(1)} %collective-permute-done.4, bf16[6,8,128,256]{3,2,1,0:T(8,128)(2,1)S(1)} %constant_dynamic-update-slice_fusion, bf16[4,8,128,128]{3,2,1,0:T(8,128)(2,1)S(1)} %bitcast.88, pred[4,8]{1,0:T(4,128)(4,1)S(1)} %get-tuple-element.54), kind=kOutput, calls=%fused_computation.50 | convolution fusion | flops 270008320 | bytes 8781856 | tf_op jit(solution)/shard_map/xynm,xymh->xynh/dot_general | solution.py:49
  61.5 7.3 %add_convert_fusion.3 = bf16[4,8,128,256]{3,2,1,0:T(8,128)(2,1)} fusion(f32[4,8,128,256]{3,2,1,0:T(8,128)} %fusion.21, f32[4,8,128,256]{3,2,1,0:T(8,128)S(1)} %fusion.23, f32[4,8,128,256]{3,2,1,0:T(8,128)S(1)} %fusion.25, f32[4,8,128,256]{3,2,1,0:T(8,128)} %fusion.47, f32[4,8,128,256]{3,2,1,0:T(8,128)S(1)} %copy-done.13, ...), kind=kOutput, calls=%fused_computation.13 | convolution fusion | flops 276299776 | bytes 27656224 | tf_op jit(solution)/shard_map/xymn,xymh->xynh/dot_general | solution.py:53
  68.8 4.4 %add_convert_fusion.2 = (bf16[4,8,128,256]{3,2,1,0:T(8,128)(2,1)S(1)}, f32[4,8,128,256]{3,2,1,0:T(8,128)}) fusion(bf16[4,8,128,256]{3,2,1,0:T(8,128)(2,1)S(1)} %copy-done.3, bf16[4,8,128,256]{3,2,1,0:T(8,128)(2,1)} %add_convert_fusion.3, bf16[256,256]{1,0:T(8,128)(2,1)S(1)} %copy-done.19), kind=kOutput, calls=%fused_computation.12 | convolution fusion | flops 540016640 | bytes 10616832 | tf_op jit(solution)/shard_map/xynh,hk->xynk/dot_general | solution.py:81
  73.2 1.4 collective-permute-start.6
  74.7 5.2 %collective-permute-start.7 = (bf16[1,8,128,256]{3,2,1,0:T(8,128)(2,1)S(1)}, bf16[1,8,128,256]{3,2,1,0:T(8,128)(2,1)S(1)}, u32[]{:S(2)}, u32[]{:S(2)}) collective-permute-start(bf16[1,8,128,256]{3,2,1,0:T(8,128)(2,1)S(1)} %get-tuple-element.49), channel_id=1, source_target_pairs={{0,2},{2,4},{4,6},{6,8},{8,10},{10,12},{12,14},{1,3},{3,5},{5,7},{... | collective-permute-start | bytes 1572872 | tf_op jit(solution)/shard_map/ppermute | solution.py:15
  80.7 3.2 %fusion.45 = f32[4,8,128,256]{3,2,1,0:T(8,128)} fusion(bf16[4,8,128,256]{3,2,1,0:T(8,128)(2,1)S(1)} %get-tuple-element.63, bf16[4,8,128,128]{2,3,1,0:T(8,128)(2,1)S(1)} %copy-done.6, pred[4,8]{1,0:T(4,128)(4,1)S(1)} %get-tuple-element.57), kind=kOutput, calls=%fused_computation.82 | convolution fusion | flops 268959744 | bytes 7340064 | tf_op jit(solution)/shard_map/xynm,xymh->xynh/dot_general | solution.py:38
  83.9 5.4 %collective-permute-done.6 = bf16[1,8,128,256]{3,2,1,0:T(8,128)(2,1)S(1)} collective-permute-done((bf16[1,8,128,256]{3,2,1,0:T(8,128)(2,1)S(1)}, bf16[1,8,128,256]{3,2,1,0:T(8,128)(2,1)S(1)}, u32[]{:S(2)}, u32[]{:S(2)}) %collective-permute-start.6) | collective-permute-done | bytes 524320 | tf_op jit(solution)/shard_map/ppermute | solution.py:17
  89.4 11.4 %collective-permute-done.7 = bf16[1,8,128,256]{3,2,1,0:T(8,128)(2,1)S(1)} collective-permute-done((bf16[1,8,128,256]{3,2,1,0:T(8,128)(2,1)S(1)}, bf16[1,8,128,256]{3,2,1,0:T(8,128)(2,1)S(1)}, u32[]{:S(2)}, u32[]{:S(2)}) %collective-permute-start.7) | collective-permute-done | bytes 524320 | tf_op jit(solution)/shard_map/ppermute | solution.py:15
  100.8 1.3 collective-permute-start.8
  102.1 3.3 %collective-permute-start.9 = (bf16[6,1,128,256]{3,2,1,0:T(8,128)(2,1)S(1)}, bf16[6,1,128,256]{3,2,1,0:T(8,128)(2,1)S(1)}, u32[]{:S(2)}, u32[]{:S(2)}) collective-permute-start(bf16[6,1,128,256]{3,2,1,0:T(8,128)(2,1)S(1)} %get-tuple-element.43), channel_id=1, source_target_pairs={{0,1},{2,3},{4,5},{6,7},{8,9},{10,11},{12,13},{14,15},{16,17},{18,... | collective-permute-start | bytes 1179656 | tf_op jit(solution)/shard_map/ppermute | solution.py:15
  107.4 2.8 %fusion.13 = f32[4,8,128,256]{3,2,1,0:T(8,128)} fusion(bf16[6,1,128,256]{3,2,1,0:T(8,128)(2,1)S(1)} %collective-permute-done.8, bf16[1,8,128,256]{3,2,1,0:T(8,128)(2,1)S(1)} %collective-permute-done.6, bf16[4,8,128,256]{3,2,1,0:T(8,128)(2,1)S(1)} %get-tuple-element.63, bf16[1,8,128,256]{3,2,1,0:T(8,128)(2,1)S(1)} %collective-permute-done.7, ...), kind=kOutput, calls=%fused_computation.36 | convolution fusion | flops 272105472 | bytes 8781856 | tf_op jit(solution)/shard_map/xynm,xymh->xynh/dot_general | solution.py:49
  110.2 4.7 %add_convert_fusion.1 = bf16[4,8,128,256]{3,2,1,0:T(8,128)(2,1)S(1)} fusion(f32[4,8,128,256]{3,2,1,0:T(8,128)} %fusion.13, f32[4,8,128,256]{3,2,1,0:T(8,128)S(1)} %fusion.15, f32[4,8,128,256]{3,2,1,0:T(8,128)S(1)} %fusion.17, f32[4,8,128,256]{3,2,1,0:T(8,128)} %fusion.45, f32[4,8,128,256]{3,2,1,0:T(8,128)S(1)} %fusion.44, ...), kind=kOutput, calls=%fused_computation.11 | convolution fusion | flops 278396928 | bytes 27656224 | tf_op jit(solution)/shard_map/xymn,xymh->xynh/dot_general | solution.py:53
  116.4 1.2 copy-done.8
  117.6 2.3 convolution_bitcast_fusion
  119.9 3.2 %convolution_convert_fusion = bf16[4,8,128,256]{3,2,1,0:T(8,128)(2,1)S(1)} fusion(bf16[256,256]{1,0:T(8,128)(2,1)S(1)} %copy-done.20, f32[4,8,128,256]{3,2,1,0:T(8,128)} %copy-done.8, f32[256]{0:T(256)S(1)} %copy-done.33, f32[4,8,128]{2,1,0:T(8,128)S(1)} %subtract_multiply_fusion), kind=kOutput, calls=%fused_computation.58 | convolution fusion | flops 543162368 | bytes 6439936 | tf_op jit(solution)/shard_map/xynk,hk->xynh/dot_general | solution.py:102
  124.2 1.4 collective-permute-start.10
  125.6 5.0 %collective-permute-start.11 = (bf16[1,8,128,256]{3,2,1,0:T(8,128)(2,1)}, bf16[1,8,128,256]{3,2,1,0:T(8,128)(2,1)S(1)}, u32[]{:S(2)}, u32[]{:S(2)}) collective-permute-start(bf16[1,8,128,256]{3,2,1,0:T(8,128)(2,1)} %get-tuple-element.47), channel_id=1, source_target_pairs={{0,2},{2,4},{4,6},{6,8},{8,10},{10,12},{12,14},{1,3},{3,5},{5,7},{... | collective-permute-start | bytes 1572872 | tf_op jit(solution)/shard_map/ppermute | solution.py:15
  130.7 2.7 %fusion.42 = f32[4,8,128,256]{3,2,1,0:T(8,128)} fusion(bf16[4,8,128,256]{3,2,1,0:T(8,128)(2,1)S(1)} %convolution_convert_fusion, bf16[4,8,128,128]{2,3,1,0:T(8,128)(2,1)S(1)} %copy-done.7, pred[4,8]{1,0:T(4,128)(4,1)S(1)} %copy-done.22), kind=kOutput, calls=%fused_computation.79 | convolution fusion | flops 268959744 | bytes 7340064 | tf_op jit(solution)/shard_map/xymn,xymh->xynh/dot_general | solution.py:39
  133.5 5.3 %fusion.43 = f32[4,8,128,256]{3,2,1,0:T(8,128)} fusion(bf16[4,8,128,256]{3,2,1,0:T(8,128)(2,1)} %copy-done.4, bf16[4,8,128,128]{2,3,1,0:T(8,128)(2,1)} %copy.13, pred[4,8]{1,0:T(4,128)(4,1)S(1)} %copy-done.22), kind=kOutput, calls=%fused_computation.80 | convolution fusion | flops 268959744 | bytes 7340064 | tf_op jit(solution)/shard_map/xynm,xymh->xynh/dot_general | solution.py:38
  138.7 1.6 collective-permute-done.10
  140.3 11.5 %collective-permute-done.11 = bf16[1,8,128,256]{3,2,1,0:T(8,128)(2,1)S(1)} collective-permute-done((bf16[1,8,128,256]{3,2,1,0:T(8,128)(2,1)}, bf16[1,8,128,256]{3,2,1,0:T(8,128)(2,1)S(1)}, u32[]{:S(2)}, u32[]{:S(2)}) %collective-permute-start.11) | collective-permute-done | bytes 524320 | tf_op jit(solution)/shard_map/ppermute | solution.py:15
  151.9 1.3 collective-permute-start.12
  153.2 3.4 %collective-permute-start.13 = (bf16[6,1,128,256]{3,2,1,0:T(8,128)(2,1)S(1)}, bf16[6,1,128,256]{3,2,1,0:T(8,128)(2,1)S(1)}, u32[]{:S(2)}, u32[]{:S(2)}) collective-permute-start(bf16[6,1,128,256]{3,2,1,0:T(8,128)(2,1)S(1)} %get-tuple-element.41), channel_id=1, source_target_pairs={{0,1},{2,3},{4,5},{6,7},{8,9},{10,11},{12,13},{14,15},{16,17},{18,... | collective-permute-start | bytes 1179656 | tf_op jit(solution)/shard_map/ppermute | solution.py:15
  156.7 2.8 %fusion.9 = f32[4,8,128,256]{3,2,1,0:T(8,128)} fusion(bf16[1,8,128,256]{3,2,1,0:T(8,128)(2,1)S(1)} %collective-permute-done.10, bf16[4,8,128,256]{3,2,1,0:T(8,128)(2,1)S(1)} %copy-done.5, bf16[4,8,128,128]{3,2,1,0:T(8,128)(2,1)S(1)} %bitcast.87, pred[4,8]{1,0:T(4,128)(4,1)S(1)} %copy-done.26), kind=kOutput, calls=%fused_computation.28 | convolution fusion | flops 270008320 | bytes 7864352 | tf_op jit(solution)/shard_map/xynm,xymh->xynh/dot_general | solution.py:41
  159.5 2.8 %fusion.7 = f32[4,8,128,256]{3,2,1,0:T(8,128)} fusion(bf16[4,8,128,256]{3,2,1,0:T(8,128)(2,1)S(1)} %copy-done.5, bf16[1,8,128,256]{3,2,1,0:T(8,128)(2,1)S(1)} %collective-permute-done.11, bf16[4,8,128,128]{2,3,1,0:T(8,128)(2,1)S(1)} %copy-done.10, pred[4,8]{1,0:T(4,128)(4,1)S(1)} %copy-done.24), kind=kOutput, calls=%fused_computation.25 | convolution fusion | flops 270008320 | bytes 7864352 | tf_op jit(solution)/shard_map/xymn,xymh->xynh/dot_general | solution.py:45
  162.3 2.9 %fusion.5 = f32[4,8,128,256]{3,2,1,0:T(8,128)} fusion(bf16[6,1,128,256]{3,2,1,0:T(8,128)(2,1)S(1)} %collective-permute-done.12, bf16[1,8,128,256]{3,2,1,0:T(8,128)(2,1)S(1)} %collective-permute-done.10, bf16[4,8,128,256]{3,2,1,0:T(8,128)(2,1)S(1)} %copy-done.5, bf16[1,8,128,256]{3,2,1,0:T(8,128)(2,1)S(1)} %collective-permute-done.11, ...), kind=kOutput, calls=%fused_computation.20 | convolution fusion | flops 272105472 | bytes 8781856 | tf_op jit(solution)/shard_map/xynm,xymh->xynh/dot_general | solution.py:49
  165.1 13.3 %fusion.28 = f32[256,256]{1,0:T(8,128)} fusion(bf16[4,8,128,256]{3,2,1,0:T(8,128)(2,1)} %add_convert_fusion.3, f32[4,8,128,256]{3,2,1,0:T(8,128)} %fusion.5, f32[4,8,128,256]{3,2,1,0:T(8,128)} %fusion.7, f32[4,8,128,256]{3,2,1,0:T(8,128)} %fusion.9, f32[4,8,128,256]{3,2,1,0:T(8,128)} %fusion.43, f32[4,8,128,256]{3,2,1,0:T(8,128)} %fusion.42, ...), kind=kOutput, calls=%fused_computation.60 | convolution fusion | flops 820510720 | bytes 32130080 | tf_op jit(solution)/shard_map/dot_general | solution.py:64
  178.5 2.9 %fusion.90 = f32[1,256,1,1]{1,0,3,2:T(1,128)S(1)} fusion(f32[4,8,128,1]{2,3,1,0:T(1,128)S(1)} %bitcast.94, bf16[4,8,128,256]{3,2,1,0:T(8,128)(2,1)S(1)} %get-tuple-element.63, f32[4,8,128,256]{3,2,1,0:T(8,128)} %copy-done.8), kind=kOutput, calls=%fused_computation.155 | convolution fusion | flops 5242880 | bytes 6308864 | tf_op jit(solution)/shard_map/xynh,xyn->h/dot_general | solution.py:91
  181.4 31.6 %psum.7 = f32[256]{0:T(256)} all-reduce(f32[256]{0:T(256)S(1)} %bitcast.97), channel_id=1, replica_groups=mesh['groups'=2,'wide'=8,'narrow'=2] {'wide','narrow'}, use_global_device_ids=true, to_apply=%region_2.4 | all-reduce | flops 256 | bytes 2048 | tf_op jit(solution)/shard_map/psum | solution.py:92
  213.0 35.9 %reduce-scatter.3.cloned.1.call-done = f32[16,256]{1,0:T(8,128)} async-done(((f32[256,256]{1,0:T(8,128)}), f32[16,256]{1,0:T(8,128)}) %reduce-scatter.3.cloned.1.call-update) | async-done | bytes 16400 | tf_op jit(solution)/shard_map/reduce_scatter | solution.py:110
  (119 shorter events, 13.8 us)
Async XLA Ops:
  7.2 17.6 %copy-start = (bf16[16,128,128]{2,1,0:T(8,128)(2,1)S(1)}, bf16[16,128,128]{2,1,0:T(8,128)(2,1)}, u32[]{:S(2)}) copy-start(bf16[16,128,128]{2,1,0:T(8,128)(2,1)} %param.17) | copy-start | bytes 1572868
  7.2 16.2 %copy-start.31 = (s32[4,8,3]{1,0,2:T(4,128)S(1)}, s32[4,8,3]{1,0,2:T(4,128)}, u32[]{:S(2)}) copy-start(s32[4,8,3]{1,0,2:T(4,128)} %param.16) | copy-start | bytes 1156
  7.2 15.0 %copy-start.35 = (bf16[256]{0:T(256)(128)(2,1)S(1)}, bf16[256]{0:T(256)(128)(2,1)}, u32[]{:S(2)}) copy-start(bf16[256]{0:T(256)(128)(2,1)} %param.20) | copy-start | bytes 1540
  7.2 205.8 %reduce-scatter.5.cloned.1.call-start = ((), (), s32[]{:S(2)}) async-start(), calls=%async_computation.3 | async-start | bytes 278528 | tf_op jit(solution)/shard_map/reduce_scatter | solution.py:99
  8.0 15.6 %collective-permute-start = (s32[8]{0:T(128)S(1)}, s32[8]{0:T(128)S(1)}, u32[]{:S(2)}, u32[]{:S(2)}) collective-permute-start(s32[8]{0:T(128)S(1)} %slice_bitcast_fusion.5), channel_id=1, source_target_pairs={{0,2},{2,4},{4,6},{6,8},{8,10},{10,12},{12,14},{1,3},{3,5},{5,7},{... | collective-permute-start | bytes 104 | tf_op jit(solution)/shard_map/ppermute | solution.py:27
  13.7 9.7 %collective-permute-start.1 = (s32[4]{0:T(128)S(1)}, s32[4]{0:T(128)S(1)}, u32[]{:S(2)}, u32[]{:S(2)}) collective-permute-start(s32[4]{0:T(128)S(1)} %slice_reduce_fusion), channel_id=1, source_target_pairs={{0,1},{2,3},{4,5},{6,7},{8,9},{10,11},{12,13},{14,15},{16,17},{18,... | collective-permute-start | bytes 56 | tf_op jit(solution)/shard_map/ppermute | solution.py:27
  17.5 31.0 %collective-permute-start.3 = (bf16[1,8,128,256]{3,2,1,0:T(8,128)(2,1)}, bf16[1,8,128,256]{3,2,1,0:T(8,128)(2,1)S(1)}, u32[]{:S(2)}, u32[]{:S(2)}) collective-permute-start(bf16[1,8,128,256]{3,2,1,0:T(8,128)(2,1)} %get-tuple-element.52), channel_id=1, source_target_pairs={{0,2},{2,4},{4,6},{6,8},{8,10},{10,12},{12,14},{1,3},{3,5},{5,7},{... | collective-permute-start | bytes 1572872 | tf_op jit(solution)/shard_map/ppermute | solution.py:15
  20.9 27.8 %collective-permute-start.2 = (bf16[1,8,128,256]{3,2,1,0:T(8,128)(2,1)}, bf16[1,8,128,256]{3,2,1,0:T(8,128)(2,1)}, u32[]{:S(2)}, u32[]{:S(2)}) collective-permute-start(bf16[1,8,128,256]{3,2,1,0:T(8,128)(2,1)} %get-tuple-element.51), channel_id=1, source_target_pairs={{2,0},{4,2},{6,4},{8,6},{10,8},{12,10},{14,12},{3,1},{5,3},{7,5},{... | collective-permute-start | bytes 1572872 | tf_op jit(solution)/shard_map/ppermute | solution.py:17
  24.5 56.1 %copy-start.21 = (pred[4,8]{1,0:T(4,128)(4,1)}, pred[4,8]{1,0:T(4,128)(4,1)S(1)}, u32[]{:S(2)}) copy-start(pred[4,8]{1,0:T(4,128)(4,1)S(1)} %get-tuple-element.57) | copy-start | bytes 100
  24.5 80.9 %copy-start.25 = (pred[4,8]{1,0:T(4,128)(4,1)}, pred[4,8]{1,0:T(4,128)(4,1)S(1)}, u32[]{:S(2)}) copy-start(pred[4,8]{1,0:T(4,128)(4,1)S(1)} %get-tuple-element.56) | copy-start | bytes 100
  24.5 81.7 %copy-start.23 = (pred[4,8]{1,0:T(4,128)(4,1)}, pred[4,8]{1,0:T(4,128)(4,1)S(1)}, u32[]{:S(2)}) copy-start(pred[4,8]{1,0:T(4,128)(4,1)S(1)} %get-tuple-element.55) | copy-start | bytes 100
  24.5 82.5 %copy-start.29 = (pred[4,8]{1,0:T(4,128)(4,1)}, pred[4,8]{1,0:T(4,128)(4,1)S(1)}, u32[]{:S(2)}) copy-start(pred[4,8]{1,0:T(4,128)(4,1)S(1)} %get-tuple-element.54) | copy-start | bytes 100
  24.8 3.9 %copy-start.2 = (bf16[4,8,128,256]{3,2,1,0:T(8,128)(2,1)S(1)}, bf16[4,8,128,256]{3,2,1,0:T(8,128)(2,1)}, u32[]{:S(2)}) copy-start(bf16[4,8,128,256]{3,2,1,0:T(8,128)(2,1)} %param.15) | copy-start | bytes 6291460
  48.7 5.6 %copy-start.9 = (bf16[4,8,128,128]{2,3,1,0:T(8,128)(2,1)S(1)}, bf16[4,8,128,128]{2,3,1,0:T(8,128)(2,1)}, u32[]{:S(2)}) copy-start(bf16[4,8,128,128]{2,3,1,0:T(8,128)(2,1)} %copy.15) | copy-start | bytes 3145732
  49.9 7.6 %copy-start.14 = (bf16[6,8,128,256]{3,2,1,0:T(8,128)(2,1)}, bf16[6,8,128,256]{3,2,1,0:T(8,128)(2,1)S(1)}, u32[]{:S(2)}) copy-start(bf16[6,8,128,256]{3,2,1,0:T(8,128)(2,1)S(1)} %constant_dynamic-update-slice_fusion) | copy-start | bytes 9437188
  49.9 7.5 %collective-permute-start.4 = (bf16[6,1,128,256]{3,2,1,0:T(8,128)(2,1)S(1)}, bf16[6,1,128,256]{3,2,1,0:T(8,128)(2,1)S(1)}, u32[]{:S(2)}, u32[]{:S(2)}) collective-permute-start(bf16[6,1,128,256]{3,2,1,0:T(8,128)(2,1)S(1)} %get-tuple-element.46), channel_id=1, source_target_pairs={{1,0},{3,2},{5,4},{7,6},{9,8},{11,10},{13,12},{15,14},{17,16},{19,... | collective-permute-start | bytes 1179656 | tf_op jit(solution)/shard_map/ppermute | solution.py:17
  51.2 9.2 %collective-permute-start.5 = (bf16[6,1,128,256]{3,2,1,0:T(8,128)(2,1)S(1)}, bf16[6,1,128,256]{3,2,1,0:T(8,128)(2,1)S(1)}, u32[]{:S(2)}, u32[]{:S(2)}) collective-permute-start(bf16[6,1,128,256]{3,2,1,0:T(8,128)(2,1)S(1)} %get-tuple-element.45), channel_id=1, source_target_pairs={{0,1},{2,3},{4,5},{6,7},{8,9},{10,11},{12,13},{14,15},{16,17},{18,... | collective-permute-start | bytes 1179656 | tf_op jit(solution)/shard_map/ppermute | solution.py:15
  55.5 1.9 copy-start.16
  57.5 3.3 %copy-start.13 = (f32[4,8,128,256]{3,2,1,0:T(8,128)S(1)}, f32[4,8,128,256]{3,2,1,0:T(8,128)}, u32[]{:S(2)}) copy-start(f32[4,8,128,256]{3,2,1,0:T(8,128)} %fusion.46) | copy-start | bytes 12582916
  57.5 4.0 %copy-start.15 = (bf16[4,8,128,128]{2,3,1,0:T(8,128)(2,1)S(1)}, bf16[4,8,128,128]{2,3,1,0:T(8,128)(2,1)}, u32[]{:S(2)}) copy-start(bf16[4,8,128,128]{2,3,1,0:T(8,128)(2,1)} %copy.16) | copy-start | bytes 3145732
  57.5 4.0 %copy-start.32 = (pred[4,8]{1,0:T(4,128)(4,1)S(1)}, pred[4,8]{1,0:T(4,128)(4,1)}, u32[]{:S(2)}) copy-start(pred[4,8]{1,0:T(4,128)(4,1)} %get-tuple-element.53) | copy-start | bytes 100
  61.5 7.3 %copy-start.3 = (bf16[4,8,128,256]{3,2,1,0:T(8,128)(2,1)S(1)}, bf16[4,8,128,256]{3,2,1,0:T(8,128)(2,1)}, u32[]{:S(2)}) copy-start(bf16[4,8,128,256]{3,2,1,0:T(8,128)(2,1)} %param.15) | copy-start | bytes 6291460
  61.5 7.3 %copy-start.19 = (bf16[256,256]{1,0:T(8,128)(2,1)S(1)}, bf16[256,256]{1,0:T(8,128)(2,1)}, u32[]{:S(2)}) copy-start(bf16[256,256]{1,0:T(8,128)(2,1)} %param.18) | copy-start | bytes 393220
  73.1 6.7 %copy-start.6 = (bf16[4,8,128,128]{2,3,1,0:T(8,128)(2,1)S(1)}, bf16[4,8,128,128]{2,3,1,0:T(8,128)(2,1)}, u32[]{:S(2)}) copy-start(bf16[4,8,128,128]{2,3,1,0:T(8,128)(2,1)} %copy.13) | copy-start | bytes 3145732
  73.2 16.1 %collective-permute-start.6 = (bf16[1,8,128,256]{3,2,1,0:T(8,128)(2,1)S(1)}, bf16[1,8,128,256]{3,2,1,0:T(8,128)(2,1)S(1)}, u32[]{:S(2)}, u32[]{:S(2)}) collective-permute-start(bf16[1,8,128,256]{3,2,1,0:T(8,128)(2,1)S(1)} %get-tuple-element.50), channel_id=1, source_target_pairs={{2,0},{4,2},{6,4},{8,6},{10,8},{12,10},{14,12},{3,1},{5,3},{7,5},{... | collective-permute-start | bytes 1572872 | tf_op jit(solution)/shard_map/ppermute | solution.py:17
  74.7 26.1 %collective-permute-start.7 = (bf16[1,8,128,256]{3,2,1,0:T(8,128)(2,1)S(1)}, bf16[1,8,128,256]{3,2,1,0:T(8,128)(2,1)S(1)}, u32[]{:S(2)}, u32[]{:S(2)}) collective-permute-start(bf16[1,8,128,256]{3,2,1,0:T(8,128)(2,1)S(1)} %get-tuple-element.49), channel_id=1, source_target_pairs={{0,2},{2,4},{4,6},{6,8},{8,10},{10,12},{12,14},{1,3},{3,5},{5,7},{... | collective-permute-start | bytes 1572872 | tf_op jit(solution)/shard_map/ppermute | solution.py:15
  100.8 6.2 %collective-permute-start.8 = (bf16[6,1,128,256]{3,2,1,0:T(8,128)(2,1)S(1)}, bf16[6,1,128,256]{3,2,1,0:T(8,128)(2,1)S(1)}, u32[]{:S(2)}, u32[]{:S(2)}) collective-permute-start(bf16[6,1,128,256]{3,2,1,0:T(8,128)(2,1)S(1)} %get-tuple-element.44), channel_id=1, source_target_pairs={{1,0},{3,2},{5,4},{7,6},{9,8},{11,10},{13,12},{15,14},{17,16},{19,... | collective-permute-start | bytes 1179656 | tf_op jit(solution)/shard_map/ppermute | solution.py:17
  102.1 8.1 %collective-permute-start.9 = (bf16[6,1,128,256]{3,2,1,0:T(8,128)(2,1)S(1)}, bf16[6,1,128,256]{3,2,1,0:T(8,128)(2,1)S(1)}, u32[]{:S(2)}, u32[]{:S(2)}) collective-permute-start(bf16[6,1,128,256]{3,2,1,0:T(8,128)(2,1)S(1)} %get-tuple-element.43), channel_id=1, source_target_pairs={{0,1},{2,3},{4,5},{6,7},{8,9},{10,11},{12,13},{14,15},{16,17},{18,... | collective-permute-start | bytes 1179656 | tf_op jit(solution)/shard_map/ppermute | solution.py:15
  110.2 4.7 %copy-start.20 = (bf16[256,256]{1,0:T(8,128)(2,1)S(1)}, bf16[256,256]{1,0:T(8,128)(2,1)}, u32[]{:S(2)}) copy-start(bf16[256,256]{1,0:T(8,128)(2,1)} %param.19) | copy-start | bytes 393220
  115.6 2.0 copy-start.8
  115.6 2.0 copy-start.33
  116.4 3.5 %copy-start.27 = (f32[1,4,8,128]{3,0,2,1:T(1,128)}, f32[1,4,8,128]{3,0,2,1:T(1,128)S(1)}, u32[]{:S(2)}) copy-start(f32[1,4,8,128]{3,0,2,1:T(1,128)S(1)} %fusion.53) | copy-start | bytes 49156
  123.1 7.6 %copy-start.4 = (bf16[4,8,128,256]{3,2,1,0:T(8,128)(2,1)}, bf16[4,8,128,256]{3,2,1,0:T(8,128)(2,1)S(1)}, u32[]{:S(2)}) copy-start(bf16[4,8,128,256]{3,2,1,0:T(8,128)(2,1)S(1)} %convolution_convert_fusion) | copy-start | bytes 6291460
  123.1 7.6 %copy-start.7 = (bf16[4,8,128,128]{2,3,1,0:T(8,128)(2,1)S(1)}, bf16[4,8,128,128]{2,3,1,0:T(8,128)(2,1)}, u32[]{:S(2)}) copy-start(bf16[4,8,128,128]{2,3,1,0:T(8,128)(2,1)} %copy.13) | copy-start | bytes 3145732
  123.1 7.6 %copy-start.22 = (pred[4,8]{1,0:T(4,128)(4,1)S(1)}, pred[4,8]{1,0:T(4,128)(4,1)}, u32[]{:S(2)}) copy-start(pred[4,8]{1,0:T(4,128)(4,1)} %copy-done.21) | copy-start | bytes 100
  124.2 16.2 %collective-permute-start.10 = (bf16[1,8,128,256]{3,2,1,0:T(8,128)(2,1)}, bf16[1,8,128,256]{3,2,1,0:T(8,128)(2,1)S(1)}, u32[]{:S(2)}, u32[]{:S(2)}) collective-permute-start(bf16[1,8,128,256]{3,2,1,0:T(8,128)(2,1)} %get-tuple-element.48), channel_id=1, source_target_pairs={{2,0},{4,2},{6,4},{8,6},{10,8},{12,10},{14,12},{3,1},{5,3},{7,5},{... | collective-permute-start | bytes 1572872 | tf_op jit(solution)/shard_map/ppermute | solution.py:17
  125.6 26.2 %collective-permute-start.11 = (bf16[1,8,128,256]{3,2,1,0:T(8,128)(2,1)}, bf16[1,8,128,256]{3,2,1,0:T(8,128)(2,1)S(1)}, u32[]{:S(2)}, u32[]{:S(2)}) collective-permute-start(bf16[1,8,128,256]{3,2,1,0:T(8,128)(2,1)} %get-tuple-element.47), channel_id=1, source_target_pairs={{0,2},{2,4},{4,6},{6,8},{8,10},{10,12},{12,14},{1,3},{3,5},{5,7},{... | collective-permute-start | bytes 1572872 | tf_op jit(solution)/shard_map/ppermute | solution.py:15
  133.4 115.5 %reduce-scatter.3.cloned.1.call-start = ((), (), s32[]{:S(2)}) async-start(), calls=%async_computation.2 | async-start | bytes 278528 | tf_op jit(solution)/shard_map/reduce_scatter | solution.py:110
  133.4 18.4 %copy-start.5 = (bf16[4,8,128,256]{3,2,1,0:T(8,128)(2,1)S(1)}, bf16[4,8,128,256]{3,2,1,0:T(8,128)(2,1)}, u32[]{:S(2)}) copy-start(bf16[4,8,128,256]{3,2,1,0:T(8,128)(2,1)} %copy-done.4) | copy-start | bytes 6291460
  138.7 18.0 %copy-start.12 = (bf16[32,128,128]{2,1,0:T(8,128)(2,1)S(1)}, bf16[32,128,128]{2,1,0:T(8,128)(2,1)}, u32[]{:S(2)}) copy-start(bf16[32,128,128]{2,1,0:T(8,128)(2,1)} %gather_fusion.1) | copy-start | bytes 3145732
  138.7 18.0 %copy-start.26 = (pred[4,8]{1,0:T(4,128)(4,1)S(1)}, pred[4,8]{1,0:T(4,128)(4,1)}, u32[]{:S(2)}) copy-start(pred[4,8]{1,0:T(4,128)(4,1)} %copy-done.25) | copy-start | bytes 100
  151.9 10.3 %collective-permute-start.12 = (bf16[6,1,128,256]{3,2,1,0:T(8,128)(2,1)S(1)}, bf16[6,1,128,256]{3,2,1,0:T(8,128)(2,1)S(1)}, u32[]{:S(2)}, u32[]{:S(2)}) collective-permute-start(bf16[6,1,128,256]{3,2,1,0:T(8,128)(2,1)S(1)} %get-tuple-element.42), channel_id=1, source_target_pairs={{1,0},{3,2},{5,4},{7,6},{9,8},{11,10},{13,12},{15,14},{17,16},{19,... | collective-permute-start | bytes 1179656 | tf_op jit(solution)/shard_map/ppermute | solution.py:17
  153.2 6.2 %copy-start.10 = (bf16[4,8,128,128]{2,3,1,0:T(8,128)(2,1)S(1)}, bf16[4,8,128,128]{2,3,1,0:T(8,128)(2,1)}, u32[]{:S(2)}) copy-start(bf16[4,8,128,128]{2,3,1,0:T(8,128)(2,1)} %copy.15) | copy-start | bytes 3145732
  153.2 6.2 %copy-start.24 = (pred[4,8]{1,0:T(4,128)(4,1)S(1)}, pred[4,8]{1,0:T(4,128)(4,1)}, u32[]{:S(2)}) copy-start(pred[4,8]{1,0:T(4,128)(4,1)} %copy-done.23) | copy-start | bytes 100
  153.2 11.9 %collective-permute-start.13 = (bf16[6,1,128,256]{3,2,1,0:T(8,128)(2,1)S(1)}, bf16[6,1,128,256]{3,2,1,0:T(8,128)(2,1)S(1)}, u32[]{:S(2)}, u32[]{:S(2)}) collective-permute-start(bf16[6,1,128,256]{3,2,1,0:T(8,128)(2,1)S(1)} %get-tuple-element.41), channel_id=1, source_target_pairs={{0,1},{2,3},{4,5},{6,7},{8,9},{10,11},{12,13},{14,15},{16,17},{18,... | collective-permute-start | bytes 1179656 | tf_op jit(solution)/shard_map/ppermute | solution.py:15
  159.5 2.8 %copy-start.18 = (bf16[32,128,128]{2,1,0:T(8,128)(2,1)S(1)}, bf16[32,128,128]{2,1,0:T(8,128)(2,1)}, u32[]{:S(2)}) copy-start(bf16[32,128,128]{2,1,0:T(8,128)(2,1)} %gather_fusion.3) | copy-start | bytes 3145732
  159.5 2.8 %copy-start.30 = (pred[4,8]{1,0:T(4,128)(4,1)S(1)}, pred[4,8]{1,0:T(4,128)(4,1)}, u32[]{:S(2)}) copy-start(pred[4,8]{1,0:T(4,128)(4,1)} %copy-done.29) | copy-start | bytes 100
  178.5 70.4 %copy-start.1 = (bf16[16,128,128]{2,1,0:T(8,128)(2,1)S(1)}, bf16[16,128,128]{2,1,0:T(8,128)(2,1)}, u32[]{:S(2)}) copy-start(bf16[16,128,128]{2,1,0:T(8,128)(2,1)} %param.17) | copy-start | bytes 1572868
  (4 other events, 4.0 us)
Sparse Core Ops, SparseCore 0:
  133.5 56.8 reduce-scatter.4
  194.5 54.3 reduce-scatter.2
where the time goes:
time: 257 us; the launch traced here: 256 us
  matrix products  78 us (30%)
  waiting for transfers between devices  65.9 us (26%)
  starting transfers between devices  37.9 us (15%)
  blocking collectives  31.6 us (12%)
  local copies, waits for them, and re-layouts  26.4 us (10%)
  between operations  14.6 us (6%)
    reduce_scatter x1, waiting for transfers between devices, per_device(): lax.psum_scatter(column_term(m_one_flat, gz_one_flat), ('wide', 'narrow')...  35.9 us
    psum x1, blocking collectives, per_device(): grad_readout = lax.psum(local_readout, ('wide', 'narrow'))  31.6 us
    ppermute x6, starting transfers between devices, extended(): lax.ppermute(tail, axis, [(i, (i + 1) % count) for i in range(ends)])  23.5 us
    ppermute x6, waiting for transfers between devices, extended(): lax.ppermute(tail, axis, [(i, (i + 1) % count) for i in range(ends)])  22.9 us
    dot_general x2, matrix products, column_term(): lax.dot_general(matrix, grads, (((0,), (0,)), ((), ())), preferred_elemen...  15.6 us
    dot_general x3, matrix products, apply_operator(): jnp.einsum('xynm,xymh->xynh', selfs, centre, preferred_element_type=jnp.f...  12.9 us
    dot_general x2, matrix products, apply_operator(): jnp.einsum('xymn,xymh->xynh', south, padded[1:-1, :-2], preferred_element...  12 us
    dot_general x3, matrix products, apply_operator(): jnp.einsum('xynm,xymh->xynh', north, padded[1:-1, 2:], preferred_element_...  8.55 us
  transfers between devices with their start and end apart: 16, of which 5 were waited for; matrix products, arithmetic and copies ran while one was open for 30% of the time, Pallas kernels for 0%

commit v1 on v0

--- a/solution.py
+++ b/solution.py
@@ -89,7 +89,8 @@
     scale = jnp.sqrt(jnp.float32(width) / jnp.float32(nodes))
     grad_pred = (pred - target) * scale
     local_readout = jnp.einsum("xynh,xyn->h", x_two.astype(jnp.float32), grad_pred)
-    grad_readout = lax.psum(local_readout, ("wide", "narrow"))
+    parts = lax.all_gather(local_readout, ("wide", "narrow"))
+    grad_readout = jnp.sum(parts, axis=0)
     grad_x_two = grad_pred[..., None] * readf
     tanh_two = jnp.tanh(z_two)
     grad_z_two = (grad_x_two * (1.0 - tanh_two * tanh_two)).astype(jnp.bfloat16)

time: 257 us -> 257 us (level)
  blocking collectives: 31.6 us -> 19.7 us
  waiting for transfers between devices: 65.9 us -> 77.3 us
    psum x1 -> x0, blocking collectives: 31.6 us -> none  [per_device(): grad_readout = lax.psum(local_readout, ('wide', 'narrow'))]
    all_gather x0 -> x1, blocking collectives: none -> 19.7 us  [per_device(): parts = lax.all_gather(local_readout, ('wide', 'narrow'))]
    reduce_scatter x1, waiting for transfers between devices: 35.9 us -> 47.2 us  [per_device(): lax.psum_scatter(column_term(m_one_flat, gz_one_flat), ('wide', 'narrow')...]
where the time goes in v1:
time: 257 us; the launch traced here: 256 us
  matrix products  78 us (30%)
  waiting for transfers between devices  77.3 us (30%)
  starting transfers between devices  37.8 us (15%)
  local copies, waits for them, and re-layouts  26.3 us (10%)
  blocking collectives  19.7 us (8%)
  between operations  14.6 us (6%)
    reduce_scatter x1, waiting for transfers between devices, per_device(): lax.psum_scatter(column_term(m_one_flat, gz_one_flat), ('wide', 'narrow')...  47.2 us
    ppermute x6, starting transfers between devices, extended(): lax.ppermute(tail, axis, [(i, (i + 1) % count) for i in range(ends)])  23.5 us
    ppermute x6, waiting for transfers between devices, extended(): lax.ppermute(tail, axis, [(i, (i + 1) % count) for i in range(ends)])  22.9 us
    all_gather x1, blocking collectives, per_device(): parts = lax.all_gather(local_readout, ('wide', 'narrow'))  19.7 us
    dot_general x2, matrix products, column_term(): lax.dot_general(matrix, grads, (((0,), (0,)), ((), ())), preferred_elemen...  15.6 us
    dot_general x3, matrix products, apply_operator(): jnp.einsum('xynm,xymh->xynh', selfs, centre, preferred_element_type=jnp.f...  12.8 us
    dot_general x2, matrix products, apply_operator(): jnp.einsum('xymn,xymh->xynh', south, padded[1:-1, :-2], preferred_element...  12 us
    dot_general x3, matrix products, apply_operator(): jnp.einsum('xynm,xymh->xynh', north, padded[1:-1, 2:], preferred_element_...  8.55 us
  transfers between devices with their start and end apart: 16, of which 5 were waited for; matrix products, arithmetic and copies ran while one was open for 30% of the time, Pallas kernels for 0%

profile of v1, /device:TPU:0, one launch (start us, length us, event | category | flops | bytes accessed | tf_op | source)
XLA Modules:
  0.0 255.8 jit_solution(6323042581942376033)
XLA Ops:
  8.0 4.9 %collective-permute-start = (s32[8]{0:T(128)S(1)}, s32[8]{0:T(128)S(1)}, u32[]{:S(2)}, u32[]{:S(2)}) collective-permute-start(s32[8]{0:T(128)S(1)} %slice_bitcast_fusion.5), channel_id=1, source_target_pairs={{0,2},{2,4},{4,6},{6,8},{8,10},{10,12},{12,14},{1,3},{3,5},{5,7},{... | collective-permute-start | bytes 104 | tf_op jit(solution)/shard_map/ppermute | solution.py:27
  13.7 1.5 collective-permute-start.1
  15.2 2.3 fusion.93
  17.5 3.4 %collective-permute-start.3 = (bf16[1,8,128,256]{3,2,1,0:T(8,128)(2,1)}, bf16[1,8,128,256]{3,2,1,0:T(8,128)(2,1)S(1)}, u32[]{:S(2)}, u32[]{:S(2)}) collective-permute-start(bf16[1,8,128,256]{3,2,1,0:T(8,128)(2,1)} %get-tuple-element.52), channel_id=1, source_target_pairs={{0,2},{2,4},{4,6},{6,8},{8,10},{10,12},{12,14},{1,3},{3,5},{5,7},{... | collective-permute-start | bytes 1572872 | tf_op jit(solution)/shard_map/ppermute | solution.py:15
  20.9 1.3 collective-permute-start.2
  24.9 1.7 gather_fusion
  26.5 2.3 copy.22
  28.8 4.0 %fusion.46 = f32[4,8,128,256]{3,2,1,0:T(8,128)} fusion(bf16[4,8,128,256]{3,2,1,0:T(8,128)(2,1)S(1)} %copy-done.2, bf16[4,8,128,128]{2,3,1,0:T(8,128)(2,1)} %copy.22, pred[4,8]{1,0:T(4,128)(4,1)S(1)} %get-tuple-element.57), kind=kOutput, calls=%fused_computation.84 | convolution fusion | flops 268959744 | bytes 7340064 | tf_op jit(solution)/shard_map/xymn,xymh->xynh/dot_general | solution.py:39
  32.8 1.6 gather_fusion.3
  34.6 1.7 gather_fusion.2
  36.3 2.3 copy.24
  38.5 1.7 gather_fusion.1
  40.2 1.7 gather_fusion.4
  41.9 2.3 copy.25
  44.2 4.4 %fusion.47 = f32[4,8,128,256]{3,2,1,0:T(8,128)} fusion(bf16[4,8,128,256]{3,2,1,0:T(8,128)(2,1)S(1)} %copy-done.2, bf16[4,8,128,128]{2,3,1,0:T(8,128)(2,1)} %copy.22, pred[4,8]{1,0:T(4,128)(4,1)S(1)} %get-tuple-element.57), kind=kOutput, calls=%fused_computation.85 | convolution fusion | flops 268959744 | bytes 7340064 | tf_op jit(solution)/shard_map/xynm,xymh->xynh/dot_general | solution.py:38
  50.0 1.3 collective-permute-start.4
  51.3 3.1 %collective-permute-start.5 = (bf16[6,1,128,256]{3,2,1,0:T(8,128)(2,1)S(1)}, bf16[6,1,128,256]{3,2,1,0:T(8,128)(2,1)S(1)}, u32[]{:S(2)}, u32[]{:S(2)}) collective-permute-start(bf16[6,1,128,256]{3,2,1,0:T(8,128)(2,1)S(1)} %get-tuple-element.45), channel_id=1, source_target_pairs={{0,1},{2,3},{4,5},{6,7},{8,9},{10,11},{12,13},{14,15},{16,17},{18,... | collective-permute-start | bytes 1179656 | tf_op jit(solution)/shard_map/ppermute | solution.py:15
  55.6 1.9 fusion.25
  57.6 2.9 %fusion.21 = f32[4,8,128,256]{3,2,1,0:T(8,128)} fusion(bf16[6,1,128,256]{3,2,1,0:T(8,128)(2,1)S(1)} %collective-permute-done.4, bf16[6,8,128,256]{3,2,1,0:T(8,128)(2,1)S(1)} %constant_dynamic-update-slice_fusion, bf16[4,8,128,128]{3,2,1,0:T(8,128)(2,1)S(1)} %bitcast.91, pred[4,8]{1,0:T(4,128)(4,1)S(1)} %get-tuple-element.54), kind=kOutput, calls=%fused_computation.50 | convolution fusion | flops 270008320 | bytes 8781856 | tf_op jit(solution)/shard_map/xynm,xymh->xynh/dot_general | solution.py:49
  61.5 7.3 %add_convert_fusion.3 = bf16[4,8,128,256]{3,2,1,0:T(8,128)(2,1)} fusion(f32[4,8,128,256]{3,2,1,0:T(8,128)} %fusion.21, f32[4,8,128,256]{3,2,1,0:T(8,128)S(1)} %fusion.23, f32[4,8,128,256]{3,2,1,0:T(8,128)S(1)} %fusion.25, f32[4,8,128,256]{3,2,1,0:T(8,128)} %fusion.47, f32[4,8,128,256]{3,2,1,0:T(8,128)S(1)} %copy-done.13, ...), kind=kOutput, calls=%fused_computation.13 | convolution fusion | flops 276299776 | bytes 27656224 | tf_op jit(solution)/shard_map/xymn,xymh->xynh/dot_general | solution.py:53
  68.8 4.3 %add_convert_fusion.2 = (bf16[4,8,128,256]{3,2,1,0:T(8,128)(2,1)S(1)}, f32[4,8,128,256]{3,2,1,0:T(8,128)}) fusion(bf16[4,8,128,256]{3,2,1,0:T(8,128)(2,1)S(1)} %copy-done.3, bf16[4,8,128,256]{3,2,1,0:T(8,128)(2,1)} %add_convert_fusion.3, bf16[256,256]{1,0:T(8,128)(2,1)S(1)} %copy-done.20), kind=kOutput, calls=%fused_computation.12 | convolution fusion | flops 540016640 | bytes 10616832 | tf_op jit(solution)/shard_map/xynh,hk->xynk/dot_general | solution.py:81
  73.3 1.4 collective-permute-start.6
  74.7 5.2 %collective-permute-start.7 = (bf16[1,8,128,256]{3,2,1,0:T(8,128)(2,1)S(1)}, bf16[1,8,128,256]{3,2,1,0:T(8,128)(2,1)S(1)}, u32[]{:S(2)}, u32[]{:S(2)}) collective-permute-start(bf16[1,8,128,256]{3,2,1,0:T(8,128)(2,1)S(1)} %get-tuple-element.49), channel_id=1, source_target_pairs={{0,2},{2,4},{4,6},{6,8},{8,10},{10,12},{12,14},{1,3},{3,5},{5,7},{... | collective-permute-start | bytes 1572872 | tf_op jit(solution)/shard_map/ppermute | solution.py:15
  80.7 3.2 %fusion.45 = f32[4,8,128,256]{3,2,1,0:T(8,128)} fusion(bf16[4,8,128,256]{3,2,1,0:T(8,128)(2,1)S(1)} %get-tuple-element.63, bf16[4,8,128,128]{2,3,1,0:T(8,128)(2,1)S(1)} %copy-done.6, pred[4,8]{1,0:T(4,128)(4,1)S(1)} %get-tuple-element.57), kind=kOutput, calls=%fused_computation.83 | convolution fusion | flops 268959744 | bytes 7340064 | tf_op jit(solution)/shard_map/xynm,xymh->xynh/dot_general | solution.py:38
  83.9 5.5 %collective-permute-done.6 = bf16[1,8,128,256]{3,2,1,0:T(8,128)(2,1)S(1)} collective-permute-done((bf16[1,8,128,256]{3,2,1,0:T(8,128)(2,1)S(1)}, bf16[1,8,128,256]{3,2,1,0:T(8,128)(2,1)S(1)}, u32[]{:S(2)}, u32[]{:S(2)}) %collective-permute-start.6) | collective-permute-done | bytes 524320 | tf_op jit(solution)/shard_map/ppermute | solution.py:17
  89.4 11.4 %collective-permute-done.7 = bf16[1,8,128,256]{3,2,1,0:T(8,128)(2,1)S(1)} collective-permute-done((bf16[1,8,128,256]{3,2,1,0:T(8,128)(2,1)S(1)}, bf16[1,8,128,256]{3,2,1,0:T(8,128)(2,1)S(1)}, u32[]{:S(2)}, u32[]{:S(2)}) %collective-permute-start.7) | collective-permute-done | bytes 524320 | tf_op jit(solution)/shard_map/ppermute | solution.py:15
  100.9 1.3 collective-permute-start.8
  102.2 3.3 %collective-permute-start.9 = (bf16[6,1,128,256]{3,2,1,0:T(8,128)(2,1)S(1)}, bf16[6,1,128,256]{3,2,1,0:T(8,128)(2,1)S(1)}, u32[]{:S(2)}, u32[]{:S(2)}) collective-permute-start(bf16[6,1,128,256]{3,2,1,0:T(8,128)(2,1)S(1)} %get-tuple-element.43), channel_id=1, source_target_pairs={{0,1},{2,3},{4,5},{6,7},{8,9},{10,11},{12,13},{14,15},{16,17},{18,... | collective-permute-start | bytes 1179656 | tf_op jit(solution)/shard_map/ppermute | solution.py:15
  107.5 2.8 %fusion.13 = f32[4,8,128,256]{3,2,1,0:T(8,128)} fusion(bf16[6,1,128,256]{3,2,1,0:T(8,128)(2,1)S(1)} %collective-permute-done.8, bf16[1,8,128,256]{3,2,1,0:T(8,128)(2,1)S(1)} %collective-permute-done.6, bf16[4,8,128,256]{3,2,1,0:T(8,128)(2,1)S(1)} %get-tuple-element.63, bf16[1,8,128,256]{3,2,1,0:T(8,128)(2,1)S(1)} %collective-permute-done.7, ...), kind=kOutput, calls=%fused_computation.36 | convolution fusion | flops 272105472 | bytes 8781856 | tf_op jit(solution)/shard_map/xynm,xymh->xynh/dot_general | solution.py:49
  110.2 4.7 %add_convert_fusion.1 = bf16[4,8,128,256]{3,2,1,0:T(8,128)(2,1)S(1)} fusion(f32[4,8,128,256]{3,2,1,0:T(8,128)} %fusion.13, f32[4,8,128,256]{3,2,1,0:T(8,128)S(1)} %fusion.15, f32[4,8,128,256]{3,2,1,0:T(8,128)S(1)} %fusion.17, f32[4,8,128,256]{3,2,1,0:T(8,128)} %fusion.45, f32[4,8,128,256]{3,2,1,0:T(8,128)S(1)} %fusion.44, ...), kind=kOutput, calls=%fused_computation.11 | convolution fusion | flops 278396928 | bytes 27656224 | tf_op jit(solution)/shard_map/xymn,xymh->xynh/dot_general | solution.py:53
  116.5 1.2 copy-done.8
  117.7 2.3 convolution_bitcast_fusion
  119.9 3.2 %convolution_convert_fusion = bf16[4,8,128,256]{3,2,1,0:T(8,128)(2,1)S(1)} fusion(bf16[256,256]{1,0:T(8,128)(2,1)S(1)} %copy-done.21, f32[4,8,128,256]{3,2,1,0:T(8,128)} %copy-done.8, f32[256]{0:T(256)S(1)} %copy-done.34, f32[4,8,128]{2,1,0:T(8,128)S(1)} %subtract_multiply_fusion), kind=kOutput, calls=%fused_computation.58 | convolution fusion | flops 543162368 | bytes 6439936 | tf_op jit(solution)/shard_map/xynk,hk->xynh/dot_general | solution.py:103
  124.2 1.4 collective-permute-start.10
  125.6 5.0 %collective-permute-start.11 = (bf16[1,8,128,256]{3,2,1,0:T(8,128)(2,1)}, bf16[1,8,128,256]{3,2,1,0:T(8,128)(2,1)S(1)}, u32[]{:S(2)}, u32[]{:S(2)}) collective-permute-start(bf16[1,8,128,256]{3,2,1,0:T(8,128)(2,1)} %get-tuple-element.47), channel_id=1, source_target_pairs={{0,2},{2,4},{4,6},{6,8},{8,10},{10,12},{12,14},{1,3},{3,5},{5,7},{... | collective-permute-start | bytes 1572872 | tf_op jit(solution)/shard_map/ppermute | solution.py:15
  130.7 2.7 %fusion.42 = f32[4,8,128,256]{3,2,1,0:T(8,128)} fusion(bf16[4,8,128,256]{3,2,1,0:T(8,128)(2,1)S(1)} %convolution_convert_fusion, bf16[4,8,128,128]{2,3,1,0:T(8,128)(2,1)S(1)} %copy-done.7, pred[4,8]{1,0:T(4,128)(4,1)S(1)} %copy-done.23), kind=kOutput, calls=%fused_computation.80 | convolution fusion | flops 268959744 | bytes 7340064 | tf_op jit(solution)/shard_map/xymn,xymh->xynh/dot_general | solution.py:39
  133.5 5.3 %fusion.43 = f32[4,8,128,256]{3,2,1,0:T(8,128)} fusion(bf16[4,8,128,256]{3,2,1,0:T(8,128)(2,1)} %copy-done.4, bf16[4,8,128,128]{2,3,1,0:T(8,128)(2,1)} %copy.22, pred[4,8]{1,0:T(4,128)(4,1)S(1)} %copy-done.23), kind=kOutput, calls=%fused_computation.81 | convolution fusion | flops 268959744 | bytes 7340064 | tf_op jit(solution)/shard_map/xynm,xymh->xynh/dot_general | solution.py:38
  138.8 1.6 collective-permute-done.10
  140.4 11.5 %collective-permute-done.11 = bf16[1,8,128,256]{3,2,1,0:T(8,128)(2,1)S(1)} collective-permute-done((bf16[1,8,128,256]{3,2,1,0:T(8,128)(2,1)}, bf16[1,8,128,256]{3,2,1,0:T(8,128)(2,1)S(1)}, u32[]{:S(2)}, u32[]{:S(2)}) %collective-permute-start.11) | collective-permute-done | bytes 524320 | tf_op jit(solution)/shard_map/ppermute | solution.py:15
  152.0 1.3 collective-permute-start.12
  153.3 3.4 %collective-permute-start.13 = (bf16[6,1,128,256]{3,2,1,0:T(8,128)(2,1)S(1)}, bf16[6,1,128,256]{3,2,1,0:T(8,128)(2,1)S(1)}, u32[]{:S(2)}, u32[]{:S(2)}) collective-permute-start(bf16[6,1,128,256]{3,2,1,0:T(8,128)(2,1)S(1)} %get-tuple-element.41), channel_id=1, source_target_pairs={{0,1},{2,3},{4,5},{6,7},{8,9},{10,11},{12,13},{14,15},{16,17},{18,... | collective-permute-start | bytes 1179656 | tf_op jit(solution)/shard_map/ppermute | solution.py:15
  156.8 2.8 %fusion.9 = f32[4,8,128,256]{3,2,1,0:T(8,128)} fusion(bf16[1,8,128,256]{3,2,1,0:T(8,128)(2,1)S(1)} %collective-permute-done.10, bf16[4,8,128,256]{3,2,1,0:T(8,128)(2,1)S(1)} %copy-done.5, bf16[4,8,128,128]{3,2,1,0:T(8,128)(2,1)S(1)} %bitcast.90, pred[4,8]{1,0:T(4,128)(4,1)S(1)} %copy-done.27), kind=kOutput, calls=%fused_computation.28 | convolution fusion | flops 270008320 | bytes 7864352 | tf_op jit(solution)/shard_map/xynm,xymh->xynh/dot_general | solution.py:41
  159.5 2.8 %fusion.7 = f32[4,8,128,256]{3,2,1,0:T(8,128)} fusion(bf16[4,8,128,256]{3,2,1,0:T(8,128)(2,1)S(1)} %copy-done.5, bf16[1,8,128,256]{3,2,1,0:T(8,128)(2,1)S(1)} %collective-permute-done.11, bf16[4,8,128,128]{2,3,1,0:T(8,128)(2,1)S(1)} %copy-done.10, pred[4,8]{1,0:T(4,128)(4,1)S(1)} %copy-done.25), kind=kOutput, calls=%fused_computation.25 | convolution fusion | flops 270008320 | bytes 7864352 | tf_op jit(solution)/shard_map/xymn,xymh->xynh/dot_general | solution.py:45
  162.3 2.9 %fusion.5 = f32[4,8,128,256]{3,2,1,0:T(8,128)} fusion(bf16[6,1,128,256]{3,2,1,0:T(8,128)(2,1)S(1)} %collective-permute-done.12, bf16[1,8,128,256]{3,2,1,0:T(8,128)(2,1)S(1)} %collective-permute-done.10, bf16[4,8,128,256]{3,2,1,0:T(8,128)(2,1)S(1)} %copy-done.5, bf16[1,8,128,256]{3,2,1,0:T(8,128)(2,1)S(1)} %collective-permute-done.11, ...), kind=kOutput, calls=%fused_computation.20 | convolution fusion | flops 272105472 | bytes 8781856 | tf_op jit(solution)/shard_map/xynm,xymh->xynh/dot_general | solution.py:49
  165.2 13.3 %fusion.28 = f32[256,256]{1,0:T(8,128)} fusion(bf16[4,8,128,256]{3,2,1,0:T(8,128)(2,1)} %add_convert_fusion.3, f32[4,8,128,256]{3,2,1,0:T(8,128)} %fusion.5, f32[4,8,128,256]{3,2,1,0:T(8,128)} %fusion.7, f32[4,8,128,256]{3,2,1,0:T(8,128)} %fusion.9, f32[4,8,128,256]{3,2,1,0:T(8,128)} %fusion.43, f32[4,8,128,256]{3,2,1,0:T(8,128)} %fusion.42, ...), kind=kOutput, calls=%fused_computation.60 | convolution fusion | flops 820510720 | bytes 32130080 | tf_op jit(solution)/shard_map/dot_general | solution.py:64
  178.5 2.9 %convolution_bitcast_fusion.1 = f32[1,1,256]{2,1,0:T(1,128)S(1)} fusion(f32[4,8,128,1]{2,3,1,0:T(1,128)S(1)} %bitcast.97, bf16[4,8,128,256]{3,2,1,0:T(8,128)(2,1)S(1)} %get-tuple-element.63, f32[4,8,128,256]{3,2,1,0:T(8,128)} %copy-done.8), kind=kOutput, calls=%fused_computation.62 | convolution fusion | flops 5242880 | bytes 6308864 | tf_op jit(solution)/shard_map/xynh,xyn->h/dot_general | solution.py:91
  181.4 19.7 %all-gather.1 = f32[16,1,256]{2,1,0:T(1,128)S(1)} all-gather(f32[1,1,256]{2,1,0:T(1,128)S(1)} %convolution_bitcast_fusion.1), channel_id=2, replica_groups=mesh['groups'=2,'wide'=8,'narrow'=2] {'wide','narrow'}, dimensions={0}, use_global_device_ids=true | all-gather | bytes 17408 | tf_op jit(solution)/shard_map/all_gather | solution.py:92
  201.7 47.2 %reduce-scatter.3.cloned.1.call-done = f32[16,256]{1,0:T(8,128)} async-done(((f32[256,256]{1,0:T(8,128)}), f32[16,256]{1,0:T(8,128)}) %reduce-scatter.3.cloned.1.call-update) | async-done | bytes 16400 | tf_op jit(solution)/shard_map/reduce_scatter | solution.py:111
  (122 shorter events, 14.4 us)
Async XLA Ops:
  7.2 17.7 %copy-start = (bf16[16,128,128]{2,1,0:T(8,128)(2,1)S(1)}, bf16[16,128,128]{2,1,0:T(8,128)(2,1)}, u32[]{:S(2)}) copy-start(bf16[16,128,128]{2,1,0:T(8,128)(2,1)} %param.17) | copy-start | bytes 1572868
  7.2 16.2 %copy-start.32 = (s32[4,8,3]{1,0,2:T(4,128)S(1)}, s32[4,8,3]{1,0,2:T(4,128)}, u32[]{:S(2)}) copy-start(s32[4,8,3]{1,0,2:T(4,128)} %param.16) | copy-start | bytes 1156
  7.2 15.0 %copy-start.36 = (bf16[256]{0:T(256)(128)(2,1)S(1)}, bf16[256]{0:T(256)(128)(2,1)}, u32[]{:S(2)}) copy-start(bf16[256]{0:T(256)(128)(2,1)} %param.20) | copy-start | bytes 1540
  7.2 194.5 %reduce-scatter.5.cloned.1.call-start = ((), (), s32[]{:S(2)}) async-start(), calls=%async_computation.3 | async-start | bytes 278528 | tf_op jit(solution)/shard_map/reduce_scatter | solution.py:100
  8.0 15.6 %collective-permute-start = (s32[8]{0:T(128)S(1)}, s32[8]{0:T(128)S(1)}, u32[]{:S(2)}, u32[]{:S(2)}) collective-permute-start(s32[8]{0:T(128)S(1)} %slice_bitcast_fusion.5), channel_id=1, source_target_pairs={{0,2},{2,4},{4,6},{6,8},{8,10},{10,12},{12,14},{1,3},{3,5},{5,7},{... | collective-permute-start | bytes 104 | tf_op jit(solution)/shard_map/ppermute | solution.py:27
  13.7 9.7 %collective-permute-start.1 = (s32[4]{0:T(128)S(1)}, s32[4]{0:T(128)S(1)}, u32[]{:S(2)}, u32[]{:S(2)}) collective-permute-start(s32[4]{0:T(128)S(1)} %slice_reduce_fusion), channel_id=1, source_target_pairs={{0,1},{2,3},{4,5},{6,7},{8,9},{10,11},{12,13},{14,15},{16,17},{18,... | collective-permute-start | bytes 56 | tf_op jit(solution)/shard_map/ppermute | solution.py:27
  17.5 31.1 %collective-permute-start.3 = (bf16[1,8,128,256]{3,2,1,0:T(8,128)(2,1)}, bf16[1,8,128,256]{3,2,1,0:T(8,128)(2,1)S(1)}, u32[]{:S(2)}, u32[]{:S(2)}) collective-permute-start(bf16[1,8,128,256]{3,2,1,0:T(8,128)(2,1)} %get-tuple-element.52), channel_id=1, source_target_pairs={{0,2},{2,4},{4,6},{6,8},{8,10},{10,12},{12,14},{1,3},{3,5},{5,7},{... | collective-permute-start | bytes 1572872 | tf_op jit(solution)/shard_map/ppermute | solution.py:15
  20.9 27.8 %collective-permute-start.2 = (bf16[1,8,128,256]{3,2,1,0:T(8,128)(2,1)}, bf16[1,8,128,256]{3,2,1,0:T(8,128)(2,1)}, u32[]{:S(2)}, u32[]{:S(2)}) collective-permute-start(bf16[1,8,128,256]{3,2,1,0:T(8,128)(2,1)} %get-tuple-element.51), channel_id=1, source_target_pairs={{2,0},{4,2},{6,4},{8,6},{10,8},{12,10},{14,12},{3,1},{5,3},{7,5},{... | collective-permute-start | bytes 1572872 | tf_op jit(solution)/shard_map/ppermute | solution.py:17
  24.6 56.1 %copy-start.22 = (pred[4,8]{1,0:T(4,128)(4,1)}, pred[4,8]{1,0:T(4,128)(4,1)S(1)}, u32[]{:S(2)}) copy-start(pred[4,8]{1,0:T(4,128)(4,1)S(1)} %get-tuple-element.57) | copy-start | bytes 100
  24.6 80.9 %copy-start.26 = (pred[4,8]{1,0:T(4,128)(4,1)}, pred[4,8]{1,0:T(4,128)(4,1)S(1)}, u32[]{:S(2)}) copy-start(pred[4,8]{1,0:T(4,128)(4,1)S(1)} %get-tuple-element.56) | copy-start | bytes 100
  24.6 81.6 %copy-start.24 = (pred[4,8]{1,0:T(4,128)(4,1)}, pred[4,8]{1,0:T(4,128)(4,1)S(1)}, u32[]{:S(2)}) copy-start(pred[4,8]{1,0:T(4,128)(4,1)S(1)} %get-tuple-element.55) | copy-start | bytes 100
  24.6 82.5 %copy-start.30 = (pred[4,8]{1,0:T(4,128)(4,1)}, pred[4,8]{1,0:T(4,128)(4,1)S(1)}, u32[]{:S(2)}) copy-start(pred[4,8]{1,0:T(4,128)(4,1)S(1)} %get-tuple-element.54) | copy-start | bytes 100
  24.8 4.0 %copy-start.2 = (bf16[4,8,128,256]{3,2,1,0:T(8,128)(2,1)S(1)}, bf16[4,8,128,256]{3,2,1,0:T(8,128)(2,1)}, u32[]{:S(2)}) copy-start(bf16[4,8,128,256]{3,2,1,0:T(8,128)(2,1)} %param.15) | copy-start | bytes 6291460
  48.7 5.6 %copy-start.9 = (bf16[4,8,128,128]{2,3,1,0:T(8,128)(2,1)S(1)}, bf16[4,8,128,128]{2,3,1,0:T(8,128)(2,1)}, u32[]{:S(2)}) copy-start(bf16[4,8,128,128]{2,3,1,0:T(8,128)(2,1)} %copy.24) | copy-start | bytes 3145732
  49.9 7.6 %copy-start.14 = (bf16[6,8,128,256]{3,2,1,0:T(8,128)(2,1)}, bf16[6,8,128,256]{3,2,1,0:T(8,128)(2,1)S(1)}, u32[]{:S(2)}) copy-start(bf16[6,8,128,256]{3,2,1,0:T(8,128)(2,1)S(1)} %constant_dynamic-update-slice_fusion) | copy-start | bytes 9437188
  50.0 7.5 %collective-permute-start.4 = (bf16[6,1,128,256]{3,2,1,0:T(8,128)(2,1)S(1)}, bf16[6,1,128,256]{3,2,1,0:T(8,128)(2,1)S(1)}, u32[]{:S(2)}, u32[]{:S(2)}) collective-permute-start(bf16[6,1,128,256]{3,2,1,0:T(8,128)(2,1)S(1)} %get-tuple-element.46), channel_id=1, source_target_pairs={{1,0},{3,2},{5,4},{7,6},{9,8},{11,10},{13,12},{15,14},{17,16},{19,... | collective-permute-start | bytes 1179656 | tf_op jit(solution)/shard_map/ppermute | solution.py:17
  51.3 9.2 %collective-permute-start.5 = (bf16[6,1,128,256]{3,2,1,0:T(8,128)(2,1)S(1)}, bf16[6,1,128,256]{3,2,1,0:T(8,128)(2,1)S(1)}, u32[]{:S(2)}, u32[]{:S(2)}) collective-permute-start(bf16[6,1,128,256]{3,2,1,0:T(8,128)(2,1)S(1)} %get-tuple-element.45), channel_id=1, source_target_pairs={{0,1},{2,3},{4,5},{6,7},{8,9},{10,11},{12,13},{14,15},{16,17},{18,... | collective-permute-start | bytes 1179656 | tf_op jit(solution)/shard_map/ppermute | solution.py:15
  57.5 3.3 %copy-start.13 = (f32[4,8,128,256]{3,2,1,0:T(8,128)S(1)}, f32[4,8,128,256]{3,2,1,0:T(8,128)}, u32[]{:S(2)}) copy-start(f32[4,8,128,256]{3,2,1,0:T(8,128)} %fusion.46) | copy-start | bytes 12582916
  57.5 4.0 %copy-start.15 = (bf16[4,8,128,128]{2,3,1,0:T(8,128)(2,1)S(1)}, bf16[4,8,128,128]{2,3,1,0:T(8,128)(2,1)}, u32[]{:S(2)}) copy-start(bf16[4,8,128,128]{2,3,1,0:T(8,128)(2,1)} %copy.25) | copy-start | bytes 3145732
  57.6 4.0 %copy-start.33 = (pred[4,8]{1,0:T(4,128)(4,1)S(1)}, pred[4,8]{1,0:T(4,128)(4,1)}, u32[]{:S(2)}) copy-start(pred[4,8]{1,0:T(4,128)(4,1)} %get-tuple-element.53) | copy-start | bytes 100
  61.5 7.3 %copy-start.3 = (bf16[4,8,128,256]{3,2,1,0:T(8,128)(2,1)S(1)}, bf16[4,8,128,256]{3,2,1,0:T(8,128)(2,1)}, u32[]{:S(2)}) copy-start(bf16[4,8,128,256]{3,2,1,0:T(8,128)(2,1)} %param.15) | copy-start | bytes 6291460
  61.5 7.3 %copy-start.20 = (bf16[256,256]{1,0:T(8,128)(2,1)S(1)}, bf16[256,256]{1,0:T(8,128)(2,1)}, u32[]{:S(2)}) copy-start(bf16[256,256]{1,0:T(8,128)(2,1)} %param.18) | copy-start | bytes 393220
  73.2 6.7 %copy-start.6 = (bf16[4,8,128,128]{2,3,1,0:T(8,128)(2,1)S(1)}, bf16[4,8,128,128]{2,3,1,0:T(8,128)(2,1)}, u32[]{:S(2)}) copy-start(bf16[4,8,128,128]{2,3,1,0:T(8,128)(2,1)} %copy.22) | copy-start | bytes 3145732
  73.3 16.1 %collective-permute-start.6 = (bf16[1,8,128,256]{3,2,1,0:T(8,128)(2,1)S(1)}, bf16[1,8,128,256]{3,2,1,0:T(8,128)(2,1)S(1)}, u32[]{:S(2)}, u32[]{:S(2)}) collective-permute-start(bf16[1,8,128,256]{3,2,1,0:T(8,128)(2,1)S(1)} %get-tuple-element.50), channel_id=1, source_target_pairs={{2,0},{4,2},{6,4},{8,6},{10,8},{12,10},{14,12},{3,1},{5,3},{7,5},{... | collective-permute-start | bytes 1572872 | tf_op jit(solution)/shard_map/ppermute | solution.py:17
  74.7 26.1 %collective-permute-start.7 = (bf16[1,8,128,256]{3,2,1,0:T(8,128)(2,1)S(1)}, bf16[1,8,128,256]{3,2,1,0:T(8,128)(2,1)S(1)}, u32[]{:S(2)}, u32[]{:S(2)}) collective-permute-start(bf16[1,8,128,256]{3,2,1,0:T(8,128)(2,1)S(1)} %get-tuple-element.49), channel_id=1, source_target_pairs={{0,2},{2,4},{4,6},{6,8},{8,10},{10,12},{12,14},{1,3},{3,5},{5,7},{... | collective-permute-start | bytes 1572872 | tf_op jit(solution)/shard_map/ppermute | solution.py:15
  100.9 6.2 %collective-permute-start.8 = (bf16[6,1,128,256]{3,2,1,0:T(8,128)(2,1)S(1)}, bf16[6,1,128,256]{3,2,1,0:T(8,128)(2,1)S(1)}, u32[]{:S(2)}, u32[]{:S(2)}) collective-permute-start(bf16[6,1,128,256]{3,2,1,0:T(8,128)(2,1)S(1)} %get-tuple-element.44), channel_id=1, source_target_pairs={{1,0},{3,2},{5,4},{7,6},{9,8},{11,10},{13,12},{15,14},{17,16},{19,... | collective-permute-start | bytes 1179656 | tf_op jit(solution)/shard_map/ppermute | solution.py:17
  102.2 8.1 %collective-permute-start.9 = (bf16[6,1,128,256]{3,2,1,0:T(8,128)(2,1)S(1)}, bf16[6,1,128,256]{3,2,1,0:T(8,128)(2,1)S(1)}, u32[]{:S(2)}, u32[]{:S(2)}) collective-permute-start(bf16[6,1,128,256]{3,2,1,0:T(8,128)(2,1)S(1)} %get-tuple-element.43), channel_id=1, source_target_pairs={{0,1},{2,3},{4,5},{6,7},{8,9},{10,11},{12,13},{14,15},{16,17},{18,... | collective-permute-start | bytes 1179656 | tf_op jit(solution)/shard_map/ppermute | solution.py:15
  107.0 3.2 %copy-start.16 = (bf16[4,8,128,128]{2,3,1,0:T(8,128)(2,1)S(1)}, bf16[4,8,128,128]{2,3,1,0:T(8,128)(2,1)}, u32[]{:S(2)}) copy-start(bf16[4,8,128,128]{2,3,1,0:T(8,128)(2,1)} %copy.25) | copy-start | bytes 3145732
  110.2 4.7 %copy-start.21 = (bf16[256,256]{1,0:T(8,128)(2,1)S(1)}, bf16[256,256]{1,0:T(8,128)(2,1)}, u32[]{:S(2)}) copy-start(bf16[256,256]{1,0:T(8,128)(2,1)} %param.19) | copy-start | bytes 393220
  115.7 2.0 copy-start.8
  115.7 2.0 copy-start.34
  116.5 3.5 %copy-start.28 = (f32[1,4,8,128]{3,0,2,1:T(1,128)}, f32[1,4,8,128]{3,0,2,1:T(1,128)S(1)}, u32[]{:S(2)}) copy-start(f32[1,4,8,128]{3,0,2,1:T(1,128)S(1)} %fusion.53) | copy-start | bytes 49156
  123.1 7.6 %copy-start.4 = (bf16[4,8,128,256]{3,2,1,0:T(8,128)(2,1)}, bf16[4,8,128,256]{3,2,1,0:T(8,128)(2,1)S(1)}, u32[]{:S(2)}) copy-start(bf16[4,8,128,256]{3,2,1,0:T(8,128)(2,1)S(1)} %convolution_convert_fusion) | copy-start | bytes 6291460
  123.1 7.6 %copy-start.7 = (bf16[4,8,128,128]{2,3,1,0:T(8,128)(2,1)S(1)}, bf16[4,8,128,128]{2,3,1,0:T(8,128)(2,1)}, u32[]{:S(2)}) copy-start(bf16[4,8,128,128]{2,3,1,0:T(8,128)(2,1)} %copy.22) | copy-start | bytes 3145732
  123.1 7.6 %copy-start.23 = (pred[4,8]{1,0:T(4,128)(4,1)S(1)}, pred[4,8]{1,0:T(4,128)(4,1)}, u32[]{:S(2)}) copy-start(pred[4,8]{1,0:T(4,128)(4,1)} %copy-done.22) | copy-start | bytes 100
  124.2 16.2 %collective-permute-start.10 = (bf16[1,8,128,256]{3,2,1,0:T(8,128)(2,1)}, bf16[1,8,128,256]{3,2,1,0:T(8,128)(2,1)S(1)}, u32[]{:S(2)}, u32[]{:S(2)}) collective-permute-start(bf16[1,8,128,256]{3,2,1,0:T(8,128)(2,1)} %get-tuple-element.48), channel_id=1, source_target_pairs={{2,0},{4,2},{6,4},{8,6},{10,8},{12,10},{14,12},{3,1},{5,3},{7,5},{... | collective-permute-start | bytes 1572872 | tf_op jit(solution)/shard_map/ppermute | solution.py:17
  125.6 26.2 %collective-permute-start.11 = (bf16[1,8,128,256]{3,2,1,0:T(8,128)(2,1)}, bf16[1,8,128,256]{3,2,1,0:T(8,128)(2,1)S(1)}, u32[]{:S(2)}, u32[]{:S(2)}) collective-permute-start(bf16[1,8,128,256]{3,2,1,0:T(8,128)(2,1)} %get-tuple-element.47), channel_id=1, source_target_pairs={{0,2},{2,4},{4,6},{6,8},{8,10},{10,12},{12,14},{1,3},{3,5},{5,7},{... | collective-permute-start | bytes 1572872 | tf_op jit(solution)/shard_map/ppermute | solution.py:15
  133.4 115.5 %reduce-scatter.3.cloned.1.call-start = ((), (), s32[]{:S(2)}) async-start(), calls=%async_computation.2 | async-start | bytes 278528 | tf_op jit(solution)/shard_map/reduce_scatter | solution.py:111
  133.5 18.4 %copy-start.5 = (bf16[4,8,128,256]{3,2,1,0:T(8,128)(2,1)S(1)}, bf16[4,8,128,256]{3,2,1,0:T(8,128)(2,1)}, u32[]{:S(2)}) copy-start(bf16[4,8,128,256]{3,2,1,0:T(8,128)(2,1)} %copy-done.4) | copy-start | bytes 6291460
  138.8 18.0 %copy-start.12 = (bf16[32,128,128]{2,1,0:T(8,128)(2,1)S(1)}, bf16[32,128,128]{2,1,0:T(8,128)(2,1)}, u32[]{:S(2)}) copy-start(bf16[32,128,128]{2,1,0:T(8,128)(2,1)} %gather_fusion.1) | copy-start | bytes 3145732
  138.8 18.0 %copy-start.27 = (pred[4,8]{1,0:T(4,128)(4,1)S(1)}, pred[4,8]{1,0:T(4,128)(4,1)}, u32[]{:S(2)}) copy-start(pred[4,8]{1,0:T(4,128)(4,1)} %copy-done.26) | copy-start | bytes 100
  152.0 10.3 %collective-permute-start.12 = (bf16[6,1,128,256]{3,2,1,0:T(8,128)(2,1)S(1)}, bf16[6,1,128,256]{3,2,1,0:T(8,128)(2,1)S(1)}, u32[]{:S(2)}, u32[]{:S(2)}) collective-permute-start(bf16[6,1,128,256]{3,2,1,0:T(8,128)(2,1)S(1)} %get-tuple-element.42), channel_id=1, source_target_pairs={{1,0},{3,2},{5,4},{7,6},{9,8},{11,10},{13,12},{15,14},{17,16},{19,... | collective-permute-start | bytes 1179656 | tf_op jit(solution)/shard_map/ppermute | solution.py:17
  153.3 6.2 %copy-start.10 = (bf16[4,8,128,128]{2,3,1,0:T(8,128)(2,1)S(1)}, bf16[4,8,128,128]{2,3,1,0:T(8,128)(2,1)}, u32[]{:S(2)}) copy-start(bf16[4,8,128,128]{2,3,1,0:T(8,128)(2,1)} %copy.24) | copy-start | bytes 3145732
  153.3 6.2 %copy-start.25 = (pred[4,8]{1,0:T(4,128)(4,1)S(1)}, pred[4,8]{1,0:T(4,128)(4,1)}, u32[]{:S(2)}) copy-start(pred[4,8]{1,0:T(4,128)(4,1)} %copy-done.24) | copy-start | bytes 100
  153.3 11.9 %collective-permute-start.13 = (bf16[6,1,128,256]{3,2,1,0:T(8,128)(2,1)S(1)}, bf16[6,1,128,256]{3,2,1,0:T(8,128)(2,1)S(1)}, u32[]{:S(2)}, u32[]{:S(2)}) collective-permute-start(bf16[6,1,128,256]{3,2,1,0:T(8,128)(2,1)S(1)} %get-tuple-element.41), channel_id=1, source_target_pairs={{0,1},{2,3},{4,5},{6,7},{8,9},{10,11},{12,13},{14,15},{16,17},{18,... | collective-permute-start | bytes 1179656 | tf_op jit(solution)/shard_map/ppermute | solution.py:15
  159.5 2.8 %copy-start.19 = (bf16[32,128,128]{2,1,0:T(8,128)(2,1)S(1)}, bf16[32,128,128]{2,1,0:T(8,128)(2,1)}, u32[]{:S(2)}) copy-start(bf16[32,128,128]{2,1,0:T(8,128)(2,1)} %gather_fusion.3) | copy-start | bytes 3145732
  159.5 2.8 %copy-start.31 = (pred[4,8]{1,0:T(4,128)(4,1)S(1)}, pred[4,8]{1,0:T(4,128)(4,1)}, u32[]{:S(2)}) copy-start(pred[4,8]{1,0:T(4,128)(4,1)} %copy-done.30) | copy-start | bytes 100
  178.5 70.5 %copy-start.1 = (bf16[16,128,128]{2,1,0:T(8,128)(2,1)S(1)}, bf16[16,128,128]{2,1,0:T(8,128)(2,1)}, u32[]{:S(2)}) copy-start(bf16[16,128,128]{2,1,0:T(8,128)(2,1)} %param.17) | copy-start | bytes 1572868
  (5 other events, 5.9 us)
Sparse Core Ops, SparseCore 0:
  133.6 56.8 reduce-scatter.4
  194.6 54.3 reduce-scatter.2
